TPU v7x, 512 devices: a whole 4x4x16 slice. The times are simulated.
512 devices in a mesh: kpt: 16 (over x, y_lo, core), aux: 32 (over z, y_hi).
Axes of the slice: x: 4, y: 4 (y_hi: 2, y_lo: 2; y = y_hi * 2 + y_lo), z: 16, core: 2. Of those that a mesh axis runs over, the one named last changes fastest.
Arguments:
- orbitals: bfloat16 [16, 768, 384], P('kpt', 'aux'), may hold values from -6 to 6
- fitted: bfloat16 [16, 2, 64, 768, 768], P('kpt', None, 'aux'), may hold values from -0.21875 to 0.21875
- kpoint_pair_index: int32 [16, 4], P('kpt'), may hold values from 0 to 1
Outputs:
- exchange_images: float32 [2, 16, 768, 384], P(None, 'kpt', 'aux')
- orbitals_out: float32 [16, 768, 384], P('kpt', 'aux')
Inputs may be any that keep to these rules, and one draw needn't show every extreme that they name: kpoint_pair_index[k, v] names which of the 2 fitted tensors of k-point k serves visit v.
All inputs are finite; a program needn't handle non-finite values.
Results may differ from a plain program's by a relative error of at most 0.0011.
Values may be sent and summed in bfloat16 or wider, within the bound.
A program may use at most 64 MiB of HBM per device.

v0:
```python
import jax
import jax.numpy as jnp
from jax import lax
from jax.sharding import PartitionSpec as P

VISIT_COUNT = 4


update_fraction = 0.25


def passed_along(value, axis, by):
    count = lax.axis_size(axis)
    return lax.ppermute(value, axis, [(i, (i + by) % count) for i in range(count)])


def half_transform(slot_block, paired_kpoint):
    layers = slot_block.shape[0]
    flattened = slot_block.reshape(layers * slot_block.shape[1], slot_block.shape[2])
    half_done = jnp.dot(flattened, paired_kpoint, preferred_element_type=jnp.float32).astype(
        jnp.bfloat16
    )
    return half_done.reshape(layers, slot_block.shape[1], paired_kpoint.shape[1])


def on_device(orbitals, fitted, kpoint_pair_index):
    rows_here = orbitals.shape[1]
    norm_scale = 1.0 / (fitted.shape[2] * lax.axis_size("aux") * orbitals.shape[2])
    current = orbitals[0].astype(jnp.float32)
    fitted_point = fitted[0]
    applied_list = []
    for outer in range(VISIT_COUNT // 2):
        offset = outer + 1
        rounded = current.astype(jnp.bfloat16)
        own_full = lax.all_gather(rounded, "aux", axis=0, tiled=True)
        trailing = passed_along(own_full, "kpt", offset)
        leading = passed_along(own_full, "kpt", -offset)
        slot_first = lax.dynamic_index_in_dim(
            fitted_point, kpoint_pair_index[0, 2 * outer], 0, keepdims=False
        )
        slot_second = lax.dynamic_index_in_dim(
            fitted_point, kpoint_pair_index[0, 2 * outer + 1], 0, keepdims=False
        )
        half_done = jnp.concatenate(
            (half_transform(slot_first, trailing), half_transform(slot_second, leading)), axis=0
        )
        inner_block = jnp.einsum(
            "pmi,mj->pij", half_done, own_full, preferred_element_type=jnp.float32
        ).astype(jnp.bfloat16)
        partial_sum = jnp.einsum(
            "pmi,pij->mj", half_done, inner_block, preferred_element_type=jnp.float32
        )
        summed = lax.psum(partial_sum, "aux")
        applied = lax.dynamic_slice_in_dim(summed, lax.axis_index("aux") * rows_here, rows_here, 0)
        applied = applied * norm_scale
        applied_list.append(applied)
        current = current - update_fraction * applied
    return (jnp.stack(applied_list)[:, None], current[None])


def solution(mesh):
    placed = (P("kpt", "aux", None), P("kpt", None, "aux", None, None), P("kpt", None))
    return jax.shard_map(
        on_device,
        mesh=mesh,
        in_specs=placed,
        out_specs=(P(None, "kpt", "aux", None), P("kpt", "aux", None)),
        check_vma=False,
    )
```

profile of v0, /device:TPU:2, one launch (start us, length us, event | category | flops | bytes accessed | tf_op | source)
XLA Modules:
  0.0 860.0 jit_solution(11143747537137993466)
XLA Ops:
  7.2 0.0 all-reduce.3.cloned.1.call-start
  7.2 86.2 %all-gather = bf16[1,768,384]{2,1,0:T(8,128)(2,1)S(1)} all-gather(bf16[1,24,384]{2,1,0:T(8,128)(2,1)} %param.3), channel_id=2, replica_groups=mesh['kpt'=16,'aux'=32] {'aux'}, dimensions={1}, use_global_device_ids=true | all-gather | bytes 608256 | tf_op jit(solution)/shard_map/all_gather | solution.py:35
  93.4 1.9 collective-permute-start
  95.3 4.5 collective-permute-start.1
  99.9 1.5 fusion.13
  109.1 5.8 constant_dynamic-slice_fusion.1
  114.9 3.5 convolution_convert_fusion.3
  118.4 3.5 convolution_convert_fusion.2
  121.9 6.1 fusion.2
  127.9 0.0 all-reduce.3.cloned.1.call-update
  127.9 0.0 all-reduce.5.cloned.1.call-start
  128.0 304.8 %all-reduce.3.cloned.1.call-done = f32[768,384]{1,0:T(8,128)} async-done(((f32[768,384]{1,0:T(8,128)}), f32[768,384]{1,0:T(8,128)}) %all-reduce.3.cloned.1.call-update) | async-done | bytes 1179664 | tf_op jit(solution)/shard_map/psum | solution.py:53
  432.8 0.8 fusion.8
  433.6 78.8 %all_gather.7 = bf16[768,384]{1,0:T(8,128)(2,1)S(1)} all-gather(bf16[24,384]{1,0:T(8,128)(2,1)S(1)} %fusion.8), channel_id=1, replica_groups=mesh['kpt'=16,'aux'=32] {'aux'}, dimensions={0}, use_global_device_ids=true | all-gather | bytes 608256 | tf_op jit(solution)/shard_map/all_gather | solution.py:35
  512.3 4.1 collective-permute-start.2
  516.4 2.6 collective-permute-start.3
  519.1 11.1 %collective-permute-done.2 = bf16[768,384]{1,0:T(8,128)(2,1)S(1)} collective-permute-done((bf16[768,384]{1,0:T(8,128)(2,1)S(1)}, bf16[768,384]{1,0:T(8,128)(2,1)S(1)}, u32[]{:S(2)}, u32[]{:S(2)}) %collective-permute-start.2) | collective-permute-done | bytes 589856 | tf_op jit(solution)/shard_map/ppermute | solution.py:14
  530.1 4.1 convolution_convert_fusion.1
  534.2 2.5 convolution_convert_fusion
  536.7 6.0 fusion.3
  542.7 0.0 all-reduce.5.cloned.1.call-update
  542.8 308.3 %all-reduce.5.cloned.1.call-done = f32[768,384]{1,0:T(8,128)} async-done(((f32[768,384]{1,0:T(8,128)}), f32[768,384]{1,0:T(8,128)}) %all-reduce.5.cloned.1.call-update) | async-done | bytes 1179664 | tf_op jit(solution)/shard_map/psum | solution.py:53
  851.1 1.4 subtract_bitcast_fusion
  852.5 0.6 maximum_bitcast_fusion
  (5 shorter events, 0.0 us)
Async XLA Ops:
  7.2 425.6 %all-reduce.3.cloned.1.call-start = ((), (), s32[]{:S(2)}) async-start(), calls=%async_computation | async-start | bytes 2359296 | tf_op jit(solution)/shard_map/psum | solution.py:53
  93.4 21.5 %collective-permute-start = (bf16[768,384]{1,0:T(8,128)(2,1)S(1)}, bf16[768,384]{1,0:T(8,128)(2,1)}, u32[]{:S(2)}, u32[]{:S(2)}) collective-permute-start(bf16[768,384]{1,0:T(8,128)(2,1)S(1)} %bitcast.51), channel_id=1, source_target_pairs={{0,32},{32,64},{64,96},{96,128},{128,160},{160,192},{192,224},{224... | collective-permute-start | bytes 1769480 | tf_op jit(solution)/shard_map/ppermute | solution.py:14
  95.3 23.0 %collective-permute-start.1 = (bf16[768,384]{1,0:T(8,128)(2,1)S(1)}, bf16[768,384]{1,0:T(8,128)(2,1)}, u32[]{:S(2)}, u32[]{:S(2)}) collective-permute-start(bf16[768,384]{1,0:T(8,128)(2,1)S(1)} %bitcast.52), channel_id=1, source_target_pairs={{0,480},{32,0},{64,32},{96,64},{128,96},{160,128},{192,160},{224,1... | collective-permute-start | bytes 1769480 | tf_op jit(solution)/shard_map/ppermute | solution.py:14
  121.9 310.9 %copy-start = (bf16[1,24,384]{2,1,0:T(8,128)(2,1)S(1)}, bf16[1,24,384]{2,1,0:T(8,128)(2,1)}, u32[]{:S(2)}) copy-start(bf16[1,24,384]{2,1,0:T(8,128)(2,1)} %param.3) | copy-start | bytes 55300
  127.9 723.2 %all-reduce.5.cloned.1.call-start = ((), (), s32[]{:S(2)}) async-start(), calls=%async_computation.1 | async-start | bytes 2359296 | tf_op jit(solution)/shard_map/psum | solution.py:53
  512.3 17.8 %collective-permute-start.2 = (bf16[768,384]{1,0:T(8,128)(2,1)S(1)}, bf16[768,384]{1,0:T(8,128)(2,1)S(1)}, u32[]{:S(2)}, u32[]{:S(2)}) collective-permute-start(bf16[768,384]{1,0:T(8,128)(2,1)S(1)} %all_gather.7), channel_id=1, source_target_pairs={{0,64},{32,96},{64,128},{96,160},{128,192},{160,224},{192,256},{22... | collective-permute-start | bytes 1769480 | tf_op jit(solution)/shard_map/ppermute | solution.py:14
  516.4 17.8 %collective-permute-start.3 = (bf16[768,384]{1,0:T(8,128)(2,1)S(1)}, bf16[768,384]{1,0:T(8,128)(2,1)S(1)}, u32[]{:S(2)}, u32[]{:S(2)}) collective-permute-start(bf16[768,384]{1,0:T(8,128)(2,1)S(1)} %all_gather.7), channel_id=1, source_target_pairs={{0,448},{32,480},{64,0},{96,32},{128,64},{160,96},{192,128},{224,1... | collective-permute-start | bytes 1769480 | tf_op jit(solution)/shard_map/ppermute | solution.py:14
Sparse Core Ops, SparseCore 0:
  128.1 304.6 all-reduce.2
  542.9 308.1 all-reduce.4
where the time goes:
time: 861 us; the launch traced here: 860 us
  waiting for transfers between devices  624 us (72%)
  blocking collectives  165 us (19%)
  matrix products  25.7 us (3%)
  between operations  21.8 us (3%)
  starting transfers between devices  13.3 us (2%)
    psum x2, waiting for transfers between devices, on_device(): summed = lax.psum(partial_sum, 'aux')  613 us
    all_gather x2, blocking collectives, on_device(): own_full = lax.all_gather(rounded, 'aux', axis=0, tiled=True)  165 us
  transfers between devices with their start and end apart: 6, of which 3 were waited for; matrix products, arithmetic and copies ran while one was open for 2% of the time, Pallas kernels for 0%

commit v1 on v0

v1 whole, which is shorter than its diff:
```python
import functools

import jax
import jax.numpy as jnp
from jax import lax
from jax.experimental import pallas as pl
from jax.experimental.pallas import tpu as pltpu
from jax.sharding import PartitionSpec as P

MESH = pl.DeviceIdType.MESH
STEPS = 2
UPDATE = 0.25
PIECES = 3
F32, BF16 = jnp.float32, jnp.bfloat16


def kernel(
    norm,
    orb_ref,
    fit_hbm,
    idx_ref,
    ex_ref,
    out_ref,
    fit,
    pre,
    c48,
    buf,
    xs,
    bt,
    mt,
    part,
    run,
    got,
    ysend,
    yrecv,
    ap,
    fit_sem,
    pre_s,
    pre_r,
    nb_s,
    nb_r,
    ag_s,
    ag_r,
    rs_s,
    rs_r,
    y_s,
    y_r,
):
    k, a = lax.axis_index("kpt"), lax.axis_index("aux")
    nk, na = lax.axis_size("kpt"), lax.axis_size("aux")
    nz = na // 2
    right_hops, left_hops = nz // 2, nz // 2 - 1
    z, h = lax.div(a, 2), lax.rem(a, 2)
    rows, cols = buf.shape[3], buf.shape[4]
    basis = nz * rows
    piece = rows // PIECES

    def dev(dk=0, dz=0, hh=h):
        return (lax.rem(k + dk + nk, nk), lax.rem(z + dz + nz, nz) * 2 + hh)

    fetch = pltpu.make_async_copy(fit_hbm.at[0], fit, fit_sem)
    fetch.start()

    barrier = pltpu.get_barrier_semaphore()
    peers = [dev(dz=1), dev(dz=-1), dev(hh=1 - h)]
    for dk in (1, -1):
        peers += [dev(dk), dev(dk, 0, 1 - h)]
    peers += [dev(2), dev(-2)]
    for peer in peers:
        pl.semaphore_signal(barrier, inc=1, device_id=peer, device_id_type=MESH)
    pl.semaphore_wait(barrier, len(peers))

    def pre_copy(i, slot, target):
        return pltpu.make_async_remote_copy(
            src_ref=orb_ref.at[0],
            dst_ref=pre.at[slot],
            send_sem=pre_s.at[i],
            recv_sem=pre_r.at[slot],
            device_id=target,
            device_id_type=MESH,
        )

    pres = [
        pre_copy(0, 1 + h, dev(1)),
        pre_copy(1, 1 + h, dev(1, 0, 1 - h)),
        pre_copy(2, 3 + h, dev(-1)),
        pre_copy(3, 3 + h, dev(-1, 0, 1 - h)),
        pre_copy(4, 0, dev(hh=1 - h)),
    ]
    for copy in pres:
        copy.start()

    def pre_wait(slot):
        pre_copy(0, slot, dev(1)).wait_recv()

    def ag_copy(t, r, d, s, block):
        return pltpu.make_async_remote_copy(
            src_ref=buf.at[t, r, block],
            dst_ref=buf.at[t, r, block],
            send_sem=ag_s.at[d, t, r, s],
            recv_sem=ag_r.at[d, t, r, s],
            device_id=dev(dz=1 - 2 * d),
            device_id_type=MESH,
        )

    def ag_send(t, r, d, s):
        block = lax.rem(z - s + nz, nz) if d == 0 else lax.rem(z + s, nz)
        return ag_copy(t, r, d, s, block)

    def ag_wait(t, r, d, s):
        block = lax.rem(z - 1 - s + nz, nz) if d == 0 else lax.rem(z + 1 + s, nz)
        ag_copy(t, r, d, s, block).wait_recv()

    def ag_first(t, r):
        ag_send(t, r, 0, 0).start()
        ag_send(t, r, 1, 0).start()

    def ag_relay(t):
        @pl.loop(1, left_hops)
        def _(s):
            for r in range(3):
                ag_wait(t, r, 0, s - 1)
                ag_send(t, r, 0, s).start()
                ag_wait(t, r, 1, s - 1)
                ag_send(t, r, 1, s).start()

        for r in range(3):
            ag_wait(t, r, 0, right_hops - 2)
            ag_send(t, r, 0, right_hops - 1).start()

    def ag_last(t, r):
        ag_wait(t, r, 1, left_hops - 1)
        ag_wait(t, r, 0, right_hops - 1)

    def rs_copy(t, d, s, c, src):
        return pltpu.make_async_remote_copy(
            src_ref=src,
            dst_ref=got.at[t, d, s, c],
            send_sem=rs_s.at[d, t, s, c],
            recv_sem=rs_r.at[d, t, s, c],
            device_id=dev(dz=1 - 2 * d),
            device_id_type=MESH,
        )

    def rs_target(d, s):
        if d == 0:
            return lax.rem(z + right_hops - s, nz)
        return lax.rem(z - left_hops + s + nz, nz)

    def rs_first(t):
        for c in range(PIECES):
            for d in range(2):
                rs_copy(t, d, 0, c, part.at[t, rs_target(d, 0), c]).start()

    def rs_step(t, d, s, c):
        rs_copy(t, d, s - 1, c, run.at[t, d, s - 1, c]).wait_recv()
        run[t, d, s, c] = part[t, rs_target(d, s), c] + got[t, d, s - 1, c]
        rs_copy(t, d, s, c, run.at[t, d, s, c]).start()

    def y_copy(t, c):
        return pltpu.make_async_remote_copy(
            src_ref=ysend.at[t, c],
            dst_ref=yrecv.at[t, c],
            send_sem=y_s.at[t, c],
            recv_sem=y_r.at[t, c],
            device_id=dev(hh=1 - h),
            device_id_type=MESH,
        )

    def reduce(t):
        @pl.loop(1, left_hops)
        def _(s):
            for c in range(PIECES):
                for d in range(2):
                    rs_step(t, d, s, c)

        for c in range(PIECES):
            rs_step(t, 0, right_hops - 1, c)
        for c in range(PIECES):
            rs_copy(t, 1, left_hops - 1, c, run.at[t, 1, left_hops - 1, c]).wait_recv()
            rs_copy(t, 0, right_hops - 1, c, run.at[t, 0, right_hops - 1, c]).wait_recv()
            ysend[t, c] = (
                part[t, z, c]
                + got[t, 1, left_hops - 1, c]
                + got[t, 0, right_hops - 1, c]
            )
            y_copy(t, c).start()
        for c in range(PIECES):
            y_copy(t, c).wait_recv()
        total = (ysend[t] + yrecv[t]) * norm
        return total.reshape(2, rows // 2, cols)

    def nb_copy(i, r, target):
        return pltpu.make_async_remote_copy(
            src_ref=buf.at[1, 2, z],
            dst_ref=buf.at[1, r, z],
            send_sem=nb_s.at[i],
            recv_sem=nb_r.at[i],
            device_id=target,
            device_id_type=MESH,
        )

    tall = 256
    for t in range(STEPS):
        if t == 0:
            for r in range(2):
                pre_wait(1 + 2 * r)
                pre_wait(2 + 2 * r)
                both = pre[1 + 2 * r : 3 + 2 * r].astype(F32)
                buf[0, r, z] = both.reshape(rows, cols).astype(BF16)
                ag_first(0, r)
            pre_wait(0)
            c48[h] = orb_ref[0].astype(F32)
            c48[1 - h] = pre[0].astype(F32)
            buf[0, 2, z] = c48[...].reshape(rows, cols).astype(BF16)
            ag_first(0, 2)
        else:
            buf[1, 2, z] = c48[...].reshape(rows, cols).astype(BF16)
            ups = [nb_copy(0, 0, dev(2)), nb_copy(1, 1, dev(-2))]
            for copy in ups:
                copy.start()
            ag_first(1, 2)
            for r in range(2):
                ups[r].wait_recv()
                ag_first(1, r)
        ag_relay(t)
        if t == 0:
            fetch.wait()
        for v in range(2):
            ag_last(t, v)
            slot = idx_ref[0, 2 * t + v]
            for p in range(2):

                @pl.loop(0, basis // tall)
                def _(i):
                    x = jnp.dot(
                        fit[slot, p, pl.ds(i * tall, tall), :],
                        buf[t, v].reshape(basis, cols),
                        preferred_element_type=F32,
                    )
                    at = (2 * v + p) * cols
                    xs[pl.ds(i * tall, tall), at : at + cols] = x.astype(BF16)

        ag_last(t, 2)
        bt[...] = buf[t, 2].reshape(basis, cols).T
        for n in range(4):
            mt[:, n * cols : (n + 1) * cols] = jnp.dot(
                bt[...], xs[:, n * cols : (n + 1) * cols], preferred_element_type=F32
            ).astype(BF16)

        @pl.loop(0, 4)
        def _(i):
            y = lax.dot_general(
                xs[pl.ds(i * (basis // 4), basis // 4), :],
                mt[...],
                (((1,), (1,)), ((), ())),
                preferred_element_type=F32,
            )
            part[t, pl.ds(i * (nz // 4), nz // 4)] = y.reshape(
                nz // 4, PIECES, piece, cols
            )

        rs_first(t)
        applied = reduce(t)
        ap[...] = applied
        c48[...] = c48[...] - UPDATE * applied
        ex_ref[t, 0] = ap[h]
    out_ref[0] = c48[h]

    for i, copy in enumerate(pres):
        copy.wait_send()
    for copy in ups:
        copy.wait_send()
    for t in range(STEPS):
        for c in range(PIECES):
            y_copy(t, c).wait_send()

        @pl.loop(0, left_hops)
        def _(s):
            for d in range(2):
                for r in range(3):
                    ag_send(t, r, d, s).wait_send()
                for c in range(PIECES):
                    rs_copy(t, d, s, c, run.at[t, d, s, c]).wait_send()

        for r in range(3):
            ag_send(t, r, 0, right_hops - 1).wait_send()
        for c in range(PIECES):
            rs_copy(t, 0, right_hops - 1, c, run.at[t, 0, right_hops - 1, c]).wait_send()


def on_device(orbitals, fitted, kpoint_pair_index):
    _, half, cols = orbitals.shape
    _, slots, layers, basis, _ = fitted.shape
    na = lax.axis_size("aux")
    nz, rows = na // 2, 2 * half
    hops = nz // 2
    piece = rows // PIECES
    norm = 1.0 / (layers * na * cols)
    vmem = functools.partial(pl.BlockSpec, memory_space=pltpu.VMEM)
    dma = pltpu.SemaphoreType.DMA
    return pl.pallas_call(
        functools.partial(kernel, norm),
        out_shape=(
            jax.ShapeDtypeStruct((STEPS, 1, half, cols), F32),
            jax.ShapeDtypeStruct((1, half, cols), F32),
        ),
        in_specs=[
            vmem(),
            pl.BlockSpec(memory_space=pl.ANY),
            pl.BlockSpec(memory_space=pltpu.SMEM),
        ],
        out_specs=(vmem(), vmem()),
        scratch_shapes=[
            pltpu.VMEM((slots, layers, basis, basis), BF16),
            pltpu.VMEM((5, half, cols), BF16),
            pltpu.VMEM((2, half, cols), F32),
            pltpu.VMEM((STEPS, 3, nz, rows, cols), BF16),
            pltpu.VMEM((basis, 4 * cols), BF16),
            pltpu.VMEM((cols, basis), BF16),
            pltpu.VMEM((cols, 4 * cols), BF16),
            pltpu.VMEM((STEPS, nz, PIECES, piece, cols), F32),
            pltpu.VMEM((STEPS, 2, hops, PIECES, piece, cols), F32),
            pltpu.VMEM((STEPS, 2, hops, PIECES, piece, cols), F32),
            pltpu.VMEM((STEPS, PIECES, piece, cols), F32),
            pltpu.VMEM((STEPS, PIECES, piece, cols), F32),
            pltpu.VMEM((2, half, cols), F32),
            dma,
            dma((5,)),
            dma((5,)),
            dma((2,)),
            dma((2,)),
            dma((2, STEPS, 3, hops)),
            dma((2, STEPS, 3, hops)),
            dma((2, STEPS, hops, PIECES)),
            dma((2, STEPS, hops, PIECES)),
            dma((STEPS, PIECES)),
            dma((STEPS, PIECES)),
        ],
        compiler_params=pltpu.CompilerParams(
            collective_id=0, has_side_effects=True, vmem_limit_bytes=56 * 2**20
        ),
        name="exchange",
    )(orbitals, fitted, kpoint_pair_index)


def solution(mesh):
    placed = (P("kpt", "aux", None), P("kpt", None, "aux", None, None), P("kpt", None))
    return jax.shard_map(
        on_device,
        mesh=mesh,
        in_specs=placed,
        out_specs=(P(None, "kpt", "aux", None), P("kpt", "aux", None)),
        check_vma=False,
    )
```

time: 861 us -> 156 us (0.18)
  waiting for transfers between devices: 624 us -> 0 us
  blocking collectives: 165 us -> 0 us
  Pallas kernels: 0 us -> 152 us
  matrix products: 25.7 us -> 0 us
  between operations: 21.8 us -> 0.64 us
  starting transfers between devices: 13.3 us -> 0 us
    psum x2 -> x0, waiting for transfers between devices: 613 us -> none  [on_device(): summed = lax.psum(partial_sum, 'aux')]
    all_gather x2 -> x0, blocking collectives: 165 us -> none  [on_device(): own_full = lax.all_gather(rounded, 'aux', axis=0, tiled=True)]
    pallas_call x0 -> x1, Pallas kernels: none -> 152 us  [on_device(): pl.pallas_call(functools.partial(kernel, norm), out_shape=(jax.ShapeDtype...]
    dot_general x6 -> x0, matrix products: 25.7 us -> none  [the longest x4 13.6 us: half_transform(): jnp.dot(flattened, paired_kpoint, preferred_element_type=jnp.float32)]
    ppermute x4 -> x0, starting transfers between devices: 13.2 us -> none  [passed_along(): lax.ppermute(value, axis, [(i, (i + by) % count) for i in range(count)])]
    ppermute x4 -> x0, waiting for transfers between devices: 11.1 us -> none  [passed_along(): lax.ppermute(value, axis, [(i, (i + by) % count) for i in range(count)])]
  transfers between devices with their start and end apart: 6 -> 0, of which waited for: 3 -> 0; matrix products, arithmetic and copies ran while one was open for 2% -> 0% of each run, Pallas kernels for 0% -> 0%
where the time goes in v1:
time: 156 us
  Pallas kernels  152 us (97%)
  local copies, waits for them, and re-layouts  2.91 us (2%)
    pallas_call x1, Pallas kernels, on_device(): pl.pallas_call(functools.partial(kernel, norm), out_shape=(jax.ShapeDtype...  152 us

profile of v1, /device:TPU:2, one launch (start us, length us, event | category | flops | bytes accessed | tf_op | source)
XLA Modules:
  0.0 155.9 jit_solution(18275565183014663435)
XLA Ops:
  0.6 152.3 %exchange.1 = (f32[2,1,24,384]{3,2,1,0:T(8,128)}, f32[1,24,384]{2,1,0:T(8,128)}) custom-call(bf16[1,24,384]{2,1,0:T(8,128)(2,1)} %orb_ref.1, bf16[1,2,2,768,768]{4,3,2,1,0:T(8,128)(2,1)} %fit_hbm.1, s32[1,4]{1,0:T(1,128)} %idx_ref.1), custom_call_target="tpu_custom_call" | custom-call | tf_op jit(solution)/shard_map/exchange/pallas_call | solution.py:302
  153.0 1.5 copy.7
  154.5 1.4 copy.8

commit v2 on v0

v2 whole, which is shorter than its diff:
```python
import functools

import jax
import jax.numpy as jnp
from jax import lax
from jax.experimental import pallas as pl
from jax.experimental.pallas import tpu as pltpu
from jax.sharding import PartitionSpec as P

MESH = pl.DeviceIdType.MESH
STEPS = 2
UPDATE = 0.25
PIECES = 3
F32, BF16 = jnp.float32, jnp.bfloat16
GATHER_RELAYS = (0, 2, 4, 6)
REDUCE_RELAYS = (0, 2, 4, 6)


def parent(relays, distance):
    return max(r for r in relays if r < distance)


def kernel(
    norm,
    orb_ref,
    fit_hbm,
    idx_ref,
    tot_ref,
    fit,
    pre,
    c48,
    buf,
    xs,
    bt,
    mt,
    part,
    run,
    got,
    ysend,
    yrecv,
    ap,
    fit_sem,
    pre_s,
    pre_r,
    nb_s,
    nb_r,
    ag_s,
    ag_r,
    rs_s,
    rs_r,
    y_s,
    y_r,
):
    k, a = lax.axis_index("kpt"), lax.axis_index("aux")
    nk, na = lax.axis_size("kpt"), lax.axis_size("aux")
    nz = na // 2
    far = (nz // 2, nz // 2 - 1)
    z, h = lax.div(a, 2), lax.rem(a, 2)
    rows, cols = buf.shape[3], buf.shape[4]
    basis = nz * rows
    piece = rows // PIECES

    def dev(dk=0, dz=0, hh=h):
        return (lax.rem(k + dk + nk, nk), lax.rem(z + dz + nz, nz) * 2 + hh)

    def place(d, distance):
        return lax.rem(z + (1 - 2 * d) * distance + nz, nz)

    def slot_of(d, distance):
        return d * far[0] + distance - 1

    fetch = pltpu.make_async_copy(fit_hbm.at[0], fit, fit_sem)
    fetch.start()

    barrier = pltpu.get_barrier_semaphore()
    peers = [dev(hh=1 - h)] + [dev(dz=dz) for dz in (1, -1, 2, -2)]
    for dk in (1, -1, 2, -2):
        peers += [dev(dk), dev(dk, 0, 1 - h)]
    for peer in peers:
        pl.semaphore_signal(barrier, inc=1, device_id=peer, device_id_type=MESH)
    pl.semaphore_wait(barrier, len(peers))

    def remote(src, dst, send_sem, recv_sem, target):
        return pltpu.make_async_remote_copy(
            src_ref=src,
            dst_ref=dst,
            send_sem=send_sem,
            recv_sem=recv_sem,
            device_id=target,
            device_id_type=MESH,
        )

    first = remote(orb_ref.at[0], pre, pre_s, pre_r, dev(hh=1 - h))
    first.start()

    def hand(t, block):
        other = lax.rem(h + block, 2)
        src = buf.at[t, 2, block]
        for r, dk in ((0, t + 1), (1, -t - 1)):
            remote(
                src, buf.at[t, r, block], nb_s.at[t], nb_r.at[t, r], dev(dk, 0, other)
            ).start()

    def ag_send(t, d, block, at, to):
        ref = buf.at[t, 2, block]
        remote(
            ref,
            ref,
            ag_s.at[t],
            ag_r.at[t, slot_of(d, to)],
            dev(dz=(1 - 2 * d) * (to - at)),
        ).start()

    def ag_relay(t, d, at):
        block = place(1 - d, at)
        for to in range(far[d], at, -1):
            if parent(GATHER_RELAYS, to) == at:
                ag_send(t, d, block, at, to)

    def ag_wait(t, d, at):
        ref = buf.at[t, 2, place(1 - d, at)]
        remote(ref, ref, ag_s.at[t], ag_r.at[t, slot_of(d, at)], dev(dz=1)).wait_recv()

    def gather(t):
        for d in range(2):
            ag_relay(t, d, 0)
        hand(t, z)
        last = 0
        for at in GATHER_RELAYS[1:] + (far[0],):
            for d in range(2):
                if at <= far[d]:
                    ag_wait(t, d, at)
                    if at in GATHER_RELAYS:
                        ag_relay(t, d, at)
            for between in range(last + 1, at):
                for d in range(2):
                    ag_wait(t, d, between)
                    hand(t, place(1 - d, between))
            for d in range(2):
                if at <= far[d]:
                    hand(t, place(1 - d, at))
            last = at

    def nb_wait(t, r):
        ref = buf.at[t, r]
        remote(ref, ref, nb_s.at[t], nb_r.at[t, r], dev(1)).wait_recv()

    def rs_copy(t, d, at, c, src):
        to = parent(REDUCE_RELAYS, at)
        i = slot_of(d, at)
        return remote(
            src,
            got.at[t, i, c],
            rs_s.at[t],
            rs_r.at[t, i, c],
            dev(dz=(1 - 2 * d) * (at - to)),
        )

    def rs_leaf(t, at):
        for c in range(PIECES):
            for d in range(2):
                if at <= far[d]:
                    rs_copy(t, d, at, c, part.at[t, place(d, at), c]).start()

    def rs_sum(t, d, at, c):
        total = part[t, place(d, at), c]
        for child in range(far[d], at, -1):
            if parent(REDUCE_RELAYS, child) == at:
                i = slot_of(d, child)
                rs_copy(t, d, child, c, got.at[t, i, c]).wait_recv()
                total = total + got[t, i, c]
        return total

    def rs_relay(t, at):
        i = REDUCE_RELAYS.index(at) - 1

        @pl.loop(0, PIECES)
        def _(c):
            for d in range(2):
                run[t, d, i, c] = rs_sum(t, d, at, c)
                rs_copy(t, d, at, c, run.at[t, d, i, c]).start()

    def y_copy(t, c):
        return remote(
            ysend.at[t, c], yrecv.at[t, c], y_s.at[t], y_r.at[t, c], dev(hh=1 - h)
        )

    def reduce(t):
        for at in REDUCE_RELAYS[:0:-1]:
            rs_relay(t, at)
            if at - 3 > 0 and at - 3 not in REDUCE_RELAYS:
                rs_leaf(t, at - 3)

        @pl.loop(0, PIECES)
        def _(c):
            total = rs_sum(t, 0, 0, c)
            for child in range(far[1], 0, -1):
                if parent(REDUCE_RELAYS, child) == 0:
                    i = slot_of(1, child)
                    rs_copy(t, 1, child, c, got.at[t, i, c]).wait_recv()
                    total = total + got[t, i, c]
            ysend[t, c] = total
            y_copy(t, c).start()

        for c in range(PIECES):
            y_copy(t, c).wait_recv()
        return (ysend[t] + yrecv[t]).reshape(2, rows // 2, cols)

    tall = 256
    group = nz // 4
    for t in range(STEPS):
        if t == 0:
            first.wait_recv()
            c48[h] = orb_ref[0].astype(F32)
            c48[1 - h] = pre[...].astype(F32)
        buf[t, 2, z] = c48[...].reshape(rows, cols).astype(BF16)
        gather(t)
        bt[...] = buf[t, 2].reshape(basis, cols).T
        if t == 0:
            fetch.wait()
        for v in range(2):
            nb_wait(t, v)
            slot = idx_ref[0, 2 * t + v]
            for p in range(2):

                @pl.loop(0, basis // tall)
                def _(i):
                    x = jnp.dot(
                        fit[slot, p, pl.ds(i * tall, tall), :],
                        buf[t, v].reshape(basis, cols),
                        preferred_element_type=F32,
                    )
                    at = (2 * v + p) * cols
                    xs[pl.ds(i * tall, tall), at : at + cols] = x.astype(BF16)

        for n in range(4):
            mt[:, n * cols : (n + 1) * cols] = jnp.dot(
                bt[...], xs[:, n * cols : (n + 1) * cols], preferred_element_type=F32
            ).astype(BF16)

        home = lax.div(z, group) + 2
        side = jnp.where(lax.rem(z, group) * 2 >= group, 1, 3)

        def tile(i):
            y = lax.dot_general(
                xs[pl.ds(pl.multiple_of(i * (basis // 4), basis // 4), basis // 4), :],
                mt[...],
                (((1,), (1,)), ((), ())),
                preferred_element_type=F32,
            )
            part[t, pl.ds(i * group, group)] = y.reshape(group, PIECES, piece, cols)

        @pl.loop(0, 2)
        def _(i):
            tile(lax.rem(home + i * side, 4))

        rs_leaf(t, 8)
        rs_leaf(t, 7)

        @pl.loop(0, 2)
        def _(i):
            tile(lax.rem(home + 2 + i * side, 4))

        rs_leaf(t, 5)
        total = reduce(t)
        ap[...] = total
        tot_ref[t] = ap[h]
        if t < STEPS - 1:
            c48[...] = c48[...] - UPDATE * (total * norm)

    first.wait_send()
    for t in range(STEPS):
        y_all = ysend.at[t]
        remote(y_all, y_all, y_s.at[t], y_r.at[t, 0], dev(1)).wait_send()
        ring = buf.at[t, 2, pl.ds(0, nz - 1)]
        remote(ring, ring, ag_s.at[t], ag_r.at[t, 0], dev(1)).wait_send()
        handed = buf.at[t, pl.ds(0, 2)]
        remote(handed, handed, nb_s.at[t], nb_r.at[t, 0], dev(1)).wait_send()
        summed = got.at[t]
        remote(summed, summed, rs_s.at[t], rs_r.at[t, 0, 0], dev(1)).wait_send()


def on_device(orbitals, fitted, kpoint_pair_index):
    _, half, cols = orbitals.shape
    _, slots, layers, basis, _ = fitted.shape
    na = lax.axis_size("aux")
    nz, rows = na // 2, 2 * half
    piece = rows // PIECES
    norm = 1.0 / (layers * na * cols)
    relays = len(REDUCE_RELAYS) - 1
    vmem = functools.partial(pl.BlockSpec, memory_space=pltpu.VMEM)
    dma = pltpu.SemaphoreType.DMA
    totals = pl.pallas_call(
        functools.partial(kernel, norm),
        out_shape=jax.ShapeDtypeStruct((STEPS, half, cols), F32),
        in_specs=[
            vmem(),
            pl.BlockSpec(memory_space=pl.ANY),
            pl.BlockSpec(memory_space=pltpu.SMEM),
        ],
        out_specs=vmem(),
        scratch_shapes=[
            pltpu.VMEM((slots, layers, basis, basis), BF16),
            pltpu.VMEM((half, cols), BF16),
            pltpu.VMEM((2, half, cols), F32),
            pltpu.VMEM((STEPS, 3, nz, rows, cols), BF16),
            pltpu.VMEM((basis, 4 * cols), BF16),
            pltpu.VMEM((cols, basis), BF16),
            pltpu.VMEM((cols, 4 * cols), BF16),
            pltpu.VMEM((STEPS, nz, PIECES, piece, cols), F32),
            pltpu.VMEM((STEPS, 2, relays, PIECES, piece, cols), F32),
            pltpu.VMEM((STEPS, nz - 1, PIECES, piece, cols), F32),
            pltpu.VMEM((STEPS, PIECES, piece, cols), F32),
            pltpu.VMEM((STEPS, PIECES, piece, cols), F32),
            pltpu.VMEM((2, half, cols), F32),
            dma,
            dma,
            dma,
            dma((STEPS,)),
            dma((STEPS, 2)),
            dma((STEPS,)),
            dma((STEPS, nz - 1)),
            dma((STEPS,)),
            dma((STEPS, nz - 1, PIECES)),
            dma((STEPS,)),
            dma((STEPS, PIECES)),
        ],
        compiler_params=pltpu.CompilerParams(
            collective_id=0, has_side_effects=True, vmem_limit_bytes=56 * 2**20
        ),
        name="exchange",
    )(orbitals, fitted, kpoint_pair_index)
    applied = totals * norm
    current = orbitals[0].astype(F32)
    for t in range(STEPS):
        current = current - UPDATE * applied[t]
    return applied[:, None], current[None]


def solution(mesh):
    placed = (P("kpt", "aux", None), P("kpt", None, "aux", None, None), P("kpt", None))
    return jax.shard_map(
        on_device,
        mesh=mesh,
        in_specs=placed,
        out_specs=(P(None, "kpt", "aux", None), P("kpt", "aux", None)),
        check_vma=False,
    )
```

time: 861 us -> 125 us (0.15)
  waiting for transfers between devices: 624 us -> 0 us
  blocking collectives: 165 us -> 0 us
  Pallas kernels: 0 us -> 122 us
  matrix products: 25.7 us -> 0 us
  between operations: 21.8 us -> 0.65 us
  starting transfers between devices: 13.3 us -> 0 us
    psum x2 -> x0, waiting for transfers between devices: 613 us -> none  [on_device(): summed = lax.psum(partial_sum, 'aux')]
    all_gather x2 -> x0, blocking collectives: 165 us -> none  [on_device(): own_full = lax.all_gather(rounded, 'aux', axis=0, tiled=True)]
    pallas_call x0 -> x1, Pallas kernels: none -> 122 us  [on_device(): pl.pallas_call(functools.partial(kernel, norm), out_shape=jax.ShapeDtypeS...]
    dot_general x6 -> x0, matrix products: 25.7 us -> none  [the longest x4 13.6 us: half_transform(): jnp.dot(flattened, paired_kpoint, preferred_element_type=jnp.float32)]
    ppermute x4 -> x0, starting transfers between devices: 13.2 us -> none  [passed_along(): lax.ppermute(value, axis, [(i, (i + by) % count) for i in range(count)])]
    ppermute x4 -> x0, waiting for transfers between devices: 11.1 us -> none  [passed_along(): lax.ppermute(value, axis, [(i, (i + by) % count) for i in range(count)])]
  transfers between devices with their start and end apart: 6 -> 0, of which waited for: 3 -> 0; matrix products, arithmetic and copies ran while one was open for 2% -> 0% of each run, Pallas kernels for 0% -> 0%
where the time goes in v2:
time: 125 us
  Pallas kernels  122 us (98%)
  other arithmetic  2.15 us (2%)
    pallas_call x1, Pallas kernels, on_device(): pl.pallas_call(functools.partial(kernel, norm), out_shape=jax.ShapeDtypeS...  122 us

profile of v2, /device:TPU:2, one launch (start us, length us, event | category | flops | bytes accessed | tf_op | source)
XLA Modules:
  0.0 124.6 jit_solution(11414108289336961829)
XLA Ops:
  0.6 0.0 copy-start
  0.6 121.8 %exchange.1 = f32[2,24,384]{2,1,0:T(8,128)} custom-call(bf16[1,24,384]{2,1,0:T(8,128)(2,1)} %orb_ref.1, bf16[1,2,2,768,768]{4,3,2,1,0:T(8,128)(2,1)} %fit_hbm.1, s32[1,4]{1,0:T(1,128)} %idx_ref.1), custom_call_target="tpu_custom_call" | custom-call | tf_op jit(solution)/shard_map/exchange/pallas_call | solution.py:293
  122.5 1.5 %broadcast_multiply_fusion = (f32[2,24,384]{2,1,0:T(8,128)S(1)}, f32[2,1,24,384]{3,2,1,0:T(8,128)}) fusion(f32[2,24,384]{2,1,0:T(8,128)} %exchange.1), kind=kLoop, calls=%fused_computation.4 | loop fusion | flops 18432 | bytes 221184 | tf_op jit(solution)/shard_map/mul | solution.py:333
  124.0 0.0 copy-done
  124.0 0.6 fusion
Async XLA Ops:
  0.6 123.4 %copy-start = (bf16[1,24,384]{2,1,0:T(8,128)(2,1)S(1)}, bf16[1,24,384]{2,1,0:T(8,128)(2,1)}, u32[]{:S(2)}) copy-start(bf16[1,24,384]{2,1,0:T(8,128)(2,1)} %orb_ref.1) | copy-start | bytes 55300

commit v3 on v2

--- a/solution.py
+++ b/solution.py
@@ -12,8 +12,9 @@
 UPDATE = 0.25
 PIECES = 3
 F32, BF16 = jnp.float32, jnp.bfloat16
-GATHER_RELAYS = (0, 2, 4, 6)
+GATHER_RELAYS = (0, 3, 6)
 REDUCE_RELAYS = (0, 2, 4, 6)
+PEER_Z = (1, -1, 2, -2, 3, -3)
 
 
 def parent(relays, distance):
@@ -54,11 +55,13 @@
     k, a = lax.axis_index("kpt"), lax.axis_index("aux")
     nk, na = lax.axis_size("kpt"), lax.axis_size("aux")
     nz = na // 2
-    far = (nz // 2, nz // 2 - 1)
+    half = nz // 2
+    far = half - 1
     z, h = lax.div(a, 2), lax.rem(a, 2)
-    rows, cols = buf.shape[3], buf.shape[4]
+    odd = lax.rem(z, 2)
+    piece, cols = buf.shape[4], buf.shape[5]
+    rows = PIECES * piece
     basis = nz * rows
-    piece = rows // PIECES
 
     def dev(dk=0, dz=0, hh=h):
         return (lax.rem(k + dk + nk, nk), lax.rem(z + dz + nz, nz) * 2 + hh)
@@ -67,13 +70,13 @@
         return lax.rem(z + (1 - 2 * d) * distance + nz, nz)
 
     def slot_of(d, distance):
-        return d * far[0] + distance - 1
+        return nz - 2 if distance == half else d * far + distance - 1
 
     fetch = pltpu.make_async_copy(fit_hbm.at[0], fit, fit_sem)
     fetch.start()
 
     barrier = pltpu.get_barrier_semaphore()
-    peers = [dev(hh=1 - h)] + [dev(dz=dz) for dz in (1, -1, 2, -2)]
+    peers = [dev(hh=1 - h)] + [dev(dz=dz) for dz in PEER_Z]
     for dk in (1, -1, 2, -2):
         peers += [dev(dk), dev(dk, 0, 1 - h)]
     for peer in peers:
@@ -94,52 +97,68 @@
     first.start()
 
     def hand(t, block):
-        other = lax.rem(h + block, 2)
         src = buf.at[t, 2, block]
         for r, dk in ((0, t + 1), (1, -t - 1)):
+            other = lax.rem(h + block, 2)
+            if t == 0:
+                other = jnp.where(lax.rem(k + r, 2) == 0, h, other)
             remote(
                 src, buf.at[t, r, block], nb_s.at[t], nb_r.at[t, r], dev(dk, 0, other)
             ).start()
 
-    def ag_send(t, d, block, at, to):
+    def ag_edge(t, d, block, at, to, c=None):
         ref = buf.at[t, 2, block]
-        remote(
-            ref,
-            ref,
+        whole = to not in GATHER_RELAYS
+        i = slot_of(d, to)
+        return remote(
+            ref if whole else ref.at[c],
+            ref if whole else ref.at[c],
             ag_s.at[t],
-            ag_r.at[t, slot_of(d, to)],
+            ag_r.at[t, i, 0 if whole else c],
             dev(dz=(1 - 2 * d) * (to - at)),
-        ).start()
-
-    def ag_relay(t, d, at):
-        block = place(1 - d, at)
-        for to in range(far[d], at, -1):
-            if parent(GATHER_RELAYS, to) == at:
-                ag_send(t, d, block, at, to)
-
-    def ag_wait(t, d, at):
-        ref = buf.at[t, 2, place(1 - d, at)]
-        remote(ref, ref, ag_s.at[t], ag_r.at[t, slot_of(d, at)], dev(dz=1)).wait_recv()
+        )
+
+    def ag_pass(t, d, at, c):
+        for to in GATHER_RELAYS:
+            if to > at and parent(GATHER_RELAYS, to) == at:
+                ag_edge(t, d, place(1 - d, at), at, to, c).start()
+
+    def ag_leaves(t, d, at):
+        for to in range(far, at, -1):
+            if parent(GATHER_RELAYS, to) == at and to not in GATHER_RELAYS:
+                ag_edge(t, d, place(1 - d, at), at, to).start()
+
+    def ag_wait(t, d, at, c=None):
+        ag_edge(t, d, place(1 - d, at), 0, at, c).wait_recv()
 
     def gather(t):
-        for d in range(2):
-            ag_relay(t, d, 0)
-        hand(t, z)
         last = 0
-        for at in GATHER_RELAYS[1:] + (far[0],):
+        for at in GATHER_RELAYS:
+            if at > 0:
+
+                @pl.loop(0, PIECES)
+                def _(c):
+                    for d in range(2):
+                        ag_wait(t, d, at, c)
+                        ag_pass(t, d, at, c)
+
+            if at == GATHER_RELAYS[-1]:
+                ag_edge(t, odd, place(1 - odd, at), at, half).start()
             for d in range(2):
-                if at <= far[d]:
-                    ag_wait(t, d, at)
-                    if at in GATHER_RELAYS:
-                        ag_relay(t, d, at)
+                ag_leaves(t, d, at)
             for between in range(last + 1, at):
                 for d in range(2):
                     ag_wait(t, d, between)
                     hand(t, place(1 - d, between))
+            for d in range(2 if at > 0 else 1):
+                hand(t, place(1 - d, at))
+            last = at
+        for between in range(last + 1, half):
             for d in range(2):
-                if at <= far[d]:
-                    hand(t, place(1 - d, at))
-            last = at
+                ag_wait(t, d, between)
+                hand(t, place(1 - d, between))
+        ag_wait(t, 0, half)
+        hand(t, place(0, half))
 
     def nb_wait(t, r):
         ref = buf.at[t, r]
@@ -156,15 +175,24 @@
             dev(dz=(1 - 2 * d) * (at - to)),
         )
 
-    def rs_leaf(t, at):
+    def rs_leaves(t, group):
         for c in range(PIECES):
-            for d in range(2):
-                if at <= far[d]:
-                    rs_copy(t, d, at, c, part.at[t, place(d, at), c]).start()
+            for at in group:
+                if at == half:
+                    rs_copy(t, odd, at, c, part.at[t, place(0, at), c]).start()
+                else:
+                    for d in range(2):
+                        rs_copy(t, d, at, c, part.at[t, place(d, at), c]).start()
+
+    leaves = [
+        [at for at in range(half, 0, -1) if parent(REDUCE_RELAYS, at) == relay
+         and at not in REDUCE_RELAYS]
+        for relay in REDUCE_RELAYS[::-1]
+    ]
 
     def rs_sum(t, d, at, c):
         total = part[t, place(d, at), c]
-        for child in range(far[d], at, -1):
+        for child in range(far, at, -1):
             if parent(REDUCE_RELAYS, child) == at:
                 i = slot_of(d, child)
                 rs_copy(t, d, child, c, got.at[t, i, c]).wait_recv()
@@ -176,8 +204,16 @@
 
         @pl.loop(0, PIECES)
         def _(c):
+            sums = [rs_sum(t, d, at, c) for d in range(2)]
+            if at == REDUCE_RELAYS[-1]:
+                opposite = got.at[t, nz - 2, c]
+                rs_copy(t, 0, half, c, opposite).wait_recv()
+                add = opposite[...]
+                none = jnp.zeros_like(add)
+                sums[0] = sums[0] + jnp.where(odd == 0, add, none)
+                sums[1] = sums[1] + jnp.where(odd == 1, add, none)
             for d in range(2):
-                run[t, d, i, c] = rs_sum(t, d, at, c)
+                run[t, d, i, c] = sums[d]
                 rs_copy(t, d, at, c, run.at[t, d, i, c]).start()
 
     def y_copy(t, c):
@@ -186,15 +222,15 @@
         )
 
     def reduce(t):
-        for at in REDUCE_RELAYS[:0:-1]:
+        for n, at in enumerate(REDUCE_RELAYS[:0:-1]):
             rs_relay(t, at)
-            if at - 3 > 0 and at - 3 not in REDUCE_RELAYS:
-                rs_leaf(t, at - 3)
+            for leaf in leaves[n + 2 : n + 3]:
+                rs_leaves(t, leaf)
 
         @pl.loop(0, PIECES)
         def _(c):
             total = rs_sum(t, 0, 0, c)
-            for child in range(far[1], 0, -1):
+            for child in range(far, 0, -1):
                 if parent(REDUCE_RELAYS, child) == 0:
                     i = slot_of(1, child)
                     rs_copy(t, 1, child, c, got.at[t, i, c]).wait_recv()
@@ -202,23 +238,41 @@
             ysend[t, c] = total
             y_copy(t, c).start()
 
-        for c in range(PIECES):
+        @pl.loop(0, PIECES)
+        def _(c):
             y_copy(t, c).wait_recv()
-        return (ysend[t] + yrecv[t]).reshape(2, rows // 2, cols)
+            total = ysend[t, c] + yrecv[t, c]
+            here = pl.ds(pl.multiple_of(c * piece, piece), piece)
+            ap[here, :] = total
+            if t < STEPS - 1:
+                fresh = c48[here, :] - UPDATE * (total * norm)
+                c48[here, :] = fresh
+                start(t + 1, c, fresh)
+
+    def start(t, c, fresh):
+        buf[t, 2, z, c] = fresh.astype(BF16)
+        for d in range(2):
+            ag_pass(t, d, 0, c)
+
+    def half_of(which):
+        return pl.ds(pl.multiple_of(which * (rows // 2), 8), rows // 2)
 
     tall = 256
     group = nz // 4
     for t in range(STEPS):
         if t == 0:
             first.wait_recv()
-            c48[h] = orb_ref[0].astype(F32)
-            c48[1 - h] = pre[...].astype(F32)
-        buf[t, 2, z] = c48[...].reshape(rows, cols).astype(BF16)
+            c48[half_of(h), :] = orb_ref[0].astype(F32)
+            c48[half_of(1 - h), :] = pre[...].astype(F32)
+            for c in range(PIECES):
+                start(0, c, c48[c * piece : (c + 1) * piece, :])
         gather(t)
         bt[...] = buf[t, 2].reshape(basis, cols).T
         if t == 0:
             fetch.wait()
-        for v in range(2):
+        near = 1 - lax.rem(lax.div(k, t + 1), 2)
+        for n in range(2):
+            v = near if n == 0 else 1 - near
             nb_wait(t, v)
             slot = idx_ref[0, 2 * t + v]
             for p in range(2):
@@ -230,13 +284,14 @@
                         buf[t, v].reshape(basis, cols),
                         preferred_element_type=F32,
                     )
-                    at = (2 * v + p) * cols
+                    at = (2 * n + p) * cols
                     xs[pl.ds(i * tall, tall), at : at + cols] = x.astype(BF16)
 
-        for n in range(4):
-            mt[:, n * cols : (n + 1) * cols] = jnp.dot(
-                bt[...], xs[:, n * cols : (n + 1) * cols], preferred_element_type=F32
-            ).astype(BF16)
+            for m in (2 * n, 2 * n + 1):
+                at = m * cols
+                mt[:, at : at + cols] = jnp.dot(
+                    bt[...], xs[:, at : at + cols], preferred_element_type=F32
+                ).astype(BF16)
 
         home = lax.div(z, group) + 2
         side = jnp.where(lax.rem(z, group) * 2 >= group, 1, 3)
@@ -254,30 +309,35 @@
         def _(i):
             tile(lax.rem(home + i * side, 4))
 
-        rs_leaf(t, 8)
-        rs_leaf(t, 7)
+        rs_leaves(t, leaves[0])
 
         @pl.loop(0, 2)
         def _(i):
             tile(lax.rem(home + 2 + i * side, 4))
 
-        rs_leaf(t, 5)
-        total = reduce(t)
-        ap[...] = total
-        tot_ref[t] = ap[h]
-        if t < STEPS - 1:
-            c48[...] = c48[...] - UPDATE * (total * norm)
+        rs_leaves(t, leaves[1])
+        reduce(t)
+        tot_ref[t] = ap[half_of(h), :]
 
     first.wait_send()
     for t in range(STEPS):
         y_all = ysend.at[t]
         remote(y_all, y_all, y_s.at[t], y_r.at[t, 0], dev(1)).wait_send()
         ring = buf.at[t, 2, pl.ds(0, nz - 1)]
-        remote(ring, ring, ag_s.at[t], ag_r.at[t, 0], dev(1)).wait_send()
+        remote(ring, ring, ag_s.at[t], ag_r.at[t, 0, 0], dev(1)).wait_send()
         handed = buf.at[t, pl.ds(0, 2)]
         remote(handed, handed, nb_s.at[t], nb_r.at[t, 0], dev(1)).wait_send()
         summed = got.at[t]
         remote(summed, summed, rs_s.at[t], rs_r.at[t, 0, 0], dev(1)).wait_send()
+
+
+def finish(norm, tot_ref, orb_ref, ex_ref, out_ref):
+    current = orb_ref[0].astype(F32)
+    for t in range(STEPS):
+        applied = tot_ref[t] * norm
+        ex_ref[t, 0] = applied
+        current = current - UPDATE * applied
+    out_ref[0] = current
 
 
 def on_device(orbitals, fitted, kpoint_pair_index):
@@ -302,8 +362,8 @@
         scratch_shapes=[
             pltpu.VMEM((slots, layers, basis, basis), BF16),
             pltpu.VMEM((half, cols), BF16),
-            pltpu.VMEM((2, half, cols), F32),
-            pltpu.VMEM((STEPS, 3, nz, rows, cols), BF16),
+            pltpu.VMEM((rows, cols), F32),
+            pltpu.VMEM((STEPS, 3, nz, PIECES, piece, cols), BF16),
             pltpu.VMEM((basis, 4 * cols), BF16),
             pltpu.VMEM((cols, basis), BF16),
             pltpu.VMEM((cols, 4 * cols), BF16),
@@ -312,14 +372,14 @@
             pltpu.VMEM((STEPS, nz - 1, PIECES, piece, cols), F32),
             pltpu.VMEM((STEPS, PIECES, piece, cols), F32),
             pltpu.VMEM((STEPS, PIECES, piece, cols), F32),
-            pltpu.VMEM((2, half, cols), F32),
+            pltpu.VMEM((rows, cols), F32),
             dma,
             dma,
             dma,
             dma((STEPS,)),
             dma((STEPS, 2)),
             dma((STEPS,)),
-            dma((STEPS, nz - 1)),
+            dma((STEPS, nz - 1, PIECES)),
             dma((STEPS,)),
             dma((STEPS, nz - 1, PIECES)),
             dma((STEPS,)),
@@ -330,11 +390,16 @@
         ),
         name="exchange",
     )(orbitals, fitted, kpoint_pair_index)
-    applied = totals * norm
-    current = orbitals[0].astype(F32)
-    for t in range(STEPS):
-        current = current - UPDATE * applied[t]
-    return applied[:, None], current[None]
+    return pl.pallas_call(
+        functools.partial(finish, norm),
+        out_shape=(
+            jax.ShapeDtypeStruct((STEPS, 1, half, cols), F32),
+            jax.ShapeDtypeStruct((1, half, cols), F32),
+        ),
+        in_specs=[vmem(), vmem()],
+        out_specs=(vmem(), vmem()),
+        name="finish",
+    )(totals, orbitals)
 
 
 def solution(mesh):

time: 125 us -> 120 us (0.960)
  the two profiles are of different devices: /device:TPU:2 before, /device:TPU:8 now
where the time goes in v3:
time: 120 us
  Pallas kernels  119 us (99%)
    pallas_call x1, Pallas kernels, on_device(): pl.pallas_call(functools.partial(kernel, norm), out_shape=jax.ShapeDtypeS...  117 us

profile of v3, /device:TPU:8, one launch (start us, length us, event | category | flops | bytes accessed | tf_op | source)
XLA Modules:
  0.0 119.5 jit_solution(16146471466650352395)
XLA Ops:
  0.6 117.4 %exchange.1.tot_ref = f32[2,24,384]{2,1,0:T(8,128)} custom-call(bf16[1,24,384]{2,1,0:T(8,128)(2,1)} %orb_ref.3, bf16[1,2,2,768,768]{4,3,2,1,0:T(8,128)(2,1)} %fit_hbm.1, s32[1,4]{1,0:T(1,128)} %idx_ref.1), custom_call_target="tpu_custom_call" | custom-call | tf_op jit(solution)/shard_map/exchange/pallas_call | solution.py:353
  118.0 1.5 %finish.1 = (f32[2,1,24,384]{3,2,1,0:T(8,128)}, f32[1,24,384]{2,1,0:T(8,128)}) custom-call(f32[2,24,384]{2,1,0:T(8,128)} %exchange.1.tot_ref, bf16[1,24,384]{2,1,0:T(8,128)(2,1)} %orb_ref.3), custom_call_target="tpu_custom_call" | custom-call | tf_op jit(solution)/shard_map/finish/pallas_call | solution.py:393

commit v4 on v3

--- a/solution.py
+++ b/solution.py
@@ -257,7 +257,7 @@
     def half_of(which):
         return pl.ds(pl.multiple_of(which * (rows // 2), 8), rows // 2)
 
-    tall = 256
+    tall = 768
     group = nz // 4
     for t in range(STEPS):
         if t == 0:
@@ -287,11 +287,10 @@
                     at = (2 * n + p) * cols
                     xs[pl.ds(i * tall, tall), at : at + cols] = x.astype(BF16)
 
-            for m in (2 * n, 2 * n + 1):
-                at = m * cols
-                mt[:, at : at + cols] = jnp.dot(
-                    bt[...], xs[:, at : at + cols], preferred_element_type=F32
-                ).astype(BF16)
+            pair = slice(2 * n * cols, 2 * (n + 1) * cols)
+            mt[:, pair] = jnp.dot(
+                bt[...], xs[:, pair], preferred_element_type=F32
+            ).astype(BF16)
 
         home = lax.div(z, group) + 2
         side = jnp.where(lax.rem(z, group) * 2 >= group, 1, 3)

time: 120 us -> 116 us (0.967)
  Pallas kernels: 119 us -> 115 us
    pallas_call x1, Pallas kernels: 117 us -> 114 us  [on_device(): pl.pallas_call(functools.partial(kernel, norm), out_shape=jax.ShapeDtypeS...]
where the time goes in v4:
time: 116 us
  Pallas kernels  115 us (99%)
    pallas_call x1, Pallas kernels, on_device(): pl.pallas_call(functools.partial(kernel, norm), out_shape=jax.ShapeDtypeS...  114 us

profile of v4, /device:TPU:8, one launch (start us, length us, event | category | flops | bytes accessed | tf_op | source)
XLA Modules:
  0.0 115.9 jit_solution(4395697526000316212)
XLA Ops:
  0.6 113.7 %exchange.1.tot_ref = f32[2,24,384]{2,1,0:T(8,128)} custom-call(bf16[1,24,384]{2,1,0:T(8,128)(2,1)} %orb_ref.3, bf16[1,2,2,768,768]{4,3,2,1,0:T(8,128)(2,1)} %fit_hbm.1, s32[1,4]{1,0:T(1,128)} %idx_ref.1), custom_call_target="tpu_custom_call" | custom-call | tf_op jit(solution)/shard_map/exchange/pallas_call | solution.py:352
  114.4 1.5 %finish.1 = (f32[2,1,24,384]{3,2,1,0:T(8,128)}, f32[1,24,384]{2,1,0:T(8,128)}) custom-call(f32[2,24,384]{2,1,0:T(8,128)} %exchange.1.tot_ref, bf16[1,24,384]{2,1,0:T(8,128)(2,1)} %orb_ref.3), custom_call_target="tpu_custom_call" | custom-call | tf_op jit(solution)/shard_map/finish/pallas_call | solution.py:392
